TPU v7x, 512 devices: a whole 4x4x16 slice. The times are simulated.
512 devices in a mesh: dp: 32 (over x_hi, z), tm: 16 (over y, x_lo, core).
Axes of the slice: x: 4 (x_hi: 2, x_lo: 2; x = x_hi * 2 + x_lo), y: 4, z: 16, core: 2. Of those that a mesh axis runs over, the one named last changes fastest.
Arguments:
- clip_input: bfloat16 [32, 32, 256, 384], P('dp', 'tm'), may hold values from -32 to 32
- norm_gain: float32 [384], replicated, may hold values from 0.1 to 1.9
- qkv_weight: bfloat16 [384, 1152], replicated, may hold values from -2 to 2
- out_weight: bfloat16 [384, 384], replicated, may hold values from -0.3125 to 0.3125
- time_weight: bfloat16 [3, 384, 768], P(None, 'dp'), may hold values from -0.1875 to 0.1875
- upsample_cotangent: bfloat16 [32, 32, 256, 768], P('dp', 'tm'), may hold values from -6 to 6
Outputs:
- input_grad: bfloat16 [32, 32, 256, 384], P('dp', 'tm')
- qkv_grad: float32 [384, 1152], P('dp', 'tm')
All inputs are finite; a program needn't handle non-finite values.
Results may differ from a plain program's by a relative error of at most 0.024.
Values may be sent and summed in bfloat16 or wider, within the bound.
No kernel may reach another device: no remote copies, remote signals or barrier semaphores. Data moves between devices by JAX's collectives and lax.ppermute only.
A program may use at most 64 MiB of HBM per device.

v0:
```python
import math
import jax
import jax.numpy as jnp
from jax import lax
from jax.sharding import PartitionSpec as P


def passed_along(block, axis, distance):
    devices = range(lax.axis_size(axis))
    route = [(i - distance, i) for i in devices if i - distance in devices]
    return lax.ppermute(block, axis, route)


def rms_scaled(features, norm_gain):
    squares = jnp.mean(features * features, axis=-1, keepdims=True)
    return features * lax.rsqrt(squares + 1e-06) * norm_gain


def block_tail(qkv_rows, features, out_weight):
    width = features.shape[-1]
    queries = qkv_rows[..., :width]
    keys = qkv_rows[..., width : 2 * width]
    values = qkv_rows[..., 2 * width :]
    scores = jnp.einsum(
        "fqc,fkc->fqk", queries, keys, preferred_element_type=jnp.float32
    ) / math.sqrt(width)
    weights = jax.nn.softmax(scores, axis=-1).astype(jnp.bfloat16)
    mixed = jnp.einsum("fqk,fkc->fqc", weights, values, preferred_element_type=jnp.float32).astype(
        jnp.bfloat16
    )
    branch = jnp.einsum("fqc,cd->fqd", mixed, out_weight, preferred_element_type=jnp.float32)
    return (features + branch).astype(jnp.bfloat16)


def attention_grads(clip_rows, norm_gain, qkv_weight, out_weight, upstream):
    features = clip_rows.astype(jnp.float32)
    normed, pre_back = jax.vjp(lambda value: rms_scaled(value, norm_gain), features)
    normed_bf = normed.astype(jnp.bfloat16)
    qkv_rows = jnp.einsum(
        "fhc,cd->fhd", normed_bf, qkv_weight, preferred_element_type=jnp.float32
    ).astype(jnp.bfloat16)
    block_out, tail_back = jax.vjp(
        lambda first, second: block_tail(first, second, out_weight), qkv_rows, features
    )
    qkv_cot, feature_cot = tail_back(upstream)
    normed_cot = jnp.einsum("fhd,cd->fhc", qkv_cot, qkv_weight, preferred_element_type=jnp.float32)
    direct = pre_back(normed_cot)[0]
    input_grad = (feature_cot + direct).astype(jnp.bfloat16)
    return (input_grad, normed_bf, qkv_cot)


def on_device(clip_input, norm_gain, qkv_weight, out_weight, time_weight, upsample_cotangent):
    rows = clip_input[0]
    cotangent = upsample_cotangent[0]
    frames = cotangent.shape[0]
    width = rows.shape[-1]
    incoming = passed_along(cotangent, "tm", -1)
    padded = jnp.concatenate([cotangent, incoming], 0)
    piece = lax.all_gather(time_weight, "dp", axis=1, tiled=True)
    result = jnp.einsum(
        "fhd,cd->fhc", padded[2 : 2 + frames], piece[0], preferred_element_type=jnp.float32
    )
    result = result + jnp.einsum(
        "fhd,cd->fhc", padded[1 : 1 + frames], piece[1], preferred_element_type=jnp.float32
    )
    upstream = (
        result
        + jnp.einsum("fhd,cd->fhc", padded[0:frames], piece[2], preferred_element_type=jnp.float32)
    ).astype(jnp.bfloat16)
    input_grad, normed_bf, qkv_cot = attention_grads(
        rows, norm_gain, qkv_weight, out_weight, upstream
    )
    flat_normed = normed_bf.reshape(-1, width)
    flat_cot = qkv_cot.reshape(-1, 3 * width)
    shares = lax.psum_scatter(
        jnp.einsum("rc,rd->cd", flat_normed, flat_cot, preferred_element_type=jnp.float32).astype(
            jnp.bfloat16
        ),
        "dp",
        scatter_dimension=0,
        tiled=True,
    )
    qkv_grad = lax.psum_scatter(shares, "tm", scatter_dimension=1, tiled=True).astype(jnp.float32)
    return (input_grad[None], qkv_grad)


def solution(mesh):
    in_specs = (
        P("dp", "tm", None, None),
        P(),
        P(),
        P(),
        P(None, "dp", None),
        P("dp", "tm", None, None),
    )
    out_specs = (P("dp", "tm", None, None), P("dp", "tm"))
    return jax.shard_map(
        on_device, mesh=mesh, in_specs=in_specs, out_specs=out_specs, check_vma=False
    )
```

profile of v0, /device:TPU:4, one launch (start us, length us, event | category | flops | bytes accessed | tf_op | source)
XLA Modules:
  0.0 387.8 jit_solution(9534692791571639131)
XLA Ops:
  7.2 0.0 copy-start
  7.2 0.0 all-gather.2.cloned.1.call-start
  7.2 1.6 copy.10
  8.8 0.0 all-gather.2.cloned.1.call-update
  8.9 1.3 collective-permute-start
  10.2 1.3 dynamic-slice.6
  12.1 1.3 dynamic-slice.2
  14.0 1.1 fusion.16
  15.2 0.0 copy-done
  15.2 1.9 convolution_convert_fusion
  17.1 0.0 copy-start.2
  17.1 0.3 convolution_multiply_fusion.1
  17.4 0.4 fusion.38
  17.8 0.3 copy-done.2
  18.1 0.0 copy-start.3
  18.1 147.2 %all-gather.2.cloned.1.call-done = bf16[3,384,768]{2,0,1:T(4,128)(2,1)} async-done(((bf16[3,12,768]{2,0,1:T(4,128)(2,1)}), bf16[3,384,768]{2,0,1:T(4,128)(2,1)}) %all-gather.2.cloned.1.call-update) | async-done | bytes 1769488 | tf_op jit(solution)/shard_map/all_gather | solution.py:59
  165.3 6.4 %fusion.37 = (bf16[1,384,768]{2,0,1:T(2,128)(2,1)S(1)}, bf16[1,384,768]{2,0,1:T(2,128)(2,1)S(1)}, bf16[1,384,768]{2,0,1:T(2,128)(2,1)S(1)}) fusion(bf16[3,384,768]{2,0,1:T(4,128)(2,1)} %all-gather.2.cloned.1.call-done), kind=kLoop, calls=%fused_computation.61 | loop fusion | bytes 3538944 | tf_op jit(solution)/shard_map/slice | solution.py:61
  171.7 0.0 copy-done.3
  171.8 0.6 fusion.20
  172.4 0.0 collective-permute-done
  172.4 1.6 fusion.3
  174.0 0.0 copy-start.4
  174.0 1.8 fusion.9
  175.8 0.0 copy-done.4
  175.8 0.4 convolution_convert_fusion.4
  176.2 1.3 multiply_reduce_fusion
  177.5 2.1 convolution_convert_fusion.2
  179.7 2.2 convolution_convert_fusion.1
  181.8 0.0 copy-start.1
  181.8 0.0 copy-start.5
  181.8 0.0 copy-start.6
  181.9 1.1 convolution_convert_fusion.3
  182.9 0.0 copy-done.1
  183.0 0.0 copy-done.5
  183.0 0.0 copy-done.6
  183.0 1.9 fusion.2
  184.9 84.6 %fusion = bf16[16,1152]{1,0:T(8,128)(2,1)S(1)} fusion(bf16[384,1152]{1,0:T(8,128)(2,1)S(1)} %fusion.2), kind=kCustom, calls=%all-reduce-scatter | all-reduce-scatter fusion | flops 589825 | bytes 923648
  269.5 1.9 collective-permute-start.1
  271.4 1.9 collective-permute-start.2
  273.3 1.9 collective-permute-start.3
  275.3 1.9 collective-permute-start.4
  277.2 2.0 fusion.19
  279.2 8.9 %collective-permute-start.8 = (bf16[12,1152]{1,0:T(8,128)(2,1)S(1)}, bf16[12,1152]{1,0:T(8,128)(2,1)S(1)}, u32[]{:S(2)}, u32[]{:S(2)}) collective-permute-start(bf16[12,1152]{1,0:T(8,128)(2,1)S(1)} %slice.34), channel_id=1, source_target_pairs={{0,128},{16,144},{32,160},{48,176},{64,192},{80,208},{96,224},{112... | collective-permute-start | bytes 82952
  288.2 9.5 %collective-permute-done.8 = bf16[12,1152]{1,0:T(8,128)(2,1)S(1)} collective-permute-done((bf16[12,1152]{1,0:T(8,128)(2,1)S(1)}, bf16[12,1152]{1,0:T(8,128)(2,1)S(1)}, u32[]{:S(2)}, u32[]{:S(2)}) %collective-permute-start.8) | collective-permute-done | bytes 27680
  297.7 8.0 %collective-permute-start.5 = (bf16[16,1152]{1,0:T(8,128)(2,1)S(1)}, bf16[16,1152]{1,0:T(8,128)(2,1)S(1)}, u32[]{:S(2)}, u32[]{:S(2)}) collective-permute-start(bf16[16,1152]{1,0:T(8,128)(2,1)S(1)} %fusion), channel_id=1, source_target_pairs={{0,80},{16,96},{32,112},{48,128},{64,144},{80,160},{96,176},{112,1... | collective-permute-start | bytes 110600
  305.7 0.0 collective-permute-done.1
  305.7 3.3 collective-permute-start.6
  309.0 0.0 collective-permute-done.2
  309.0 1.9 collective-permute-start.7
  310.9 1.0 fusion.21
  311.9 0.0 collective-permute-done.3
  311.9 0.0 collective-permute-done.4
  312.0 0.0 collective-permute-done.5
  312.0 9.4 %collective-permute-done.6 = bf16[16,1152]{1,0:T(8,128)(2,1)S(1)} collective-permute-done((bf16[16,1152]{1,0:T(8,128)(2,1)S(1)}, bf16[16,1152]{1,0:T(8,128)(2,1)S(1)}, u32[]{:S(2)}, u32[]{:S(2)}) %collective-permute-start.6) | collective-permute-done | bytes 36896
  321.4 4.5 %collective-permute-done.7 = bf16[16,1152]{1,0:T(8,128)(2,1)S(1)} collective-permute-done((bf16[16,1152]{1,0:T(8,128)(2,1)S(1)}, bf16[16,1152]{1,0:T(8,128)(2,1)S(1)}, u32[]{:S(2)}, u32[]{:S(2)}) %collective-permute-start.7) | collective-permute-done | bytes 36896
  325.9 1.5 concatenate.4
  327.4 53.0 %all-reduce.4 = bf16[12,1152]{1,0:T(8,128)(2,1)S(1)} all-reduce(bf16[12,1152]{1,0:T(8,128)(2,1)S(1)} %constant_dynamic-slice_fusion), channel_id=3, replica_groups=mesh['dp'=32,'tm'=16] {'tm'}, use_global_device_ids=true, to_apply=%region_6.0.clone | all-reduce | flops 13824 | bytes 55296
  380.3 0.7 dynamic-slice_convert_fusion
  (6 shorter events, 0.1 us)
Async XLA Ops:
  7.2 8.0 %copy-start = (bf16[384,1152]{1,0:T(8,128)(2,1)S(1)}, bf16[384,1152]{1,0:T(8,128)(2,1)}, u32[]{:S(2)}) copy-start(bf16[384,1152]{1,0:T(8,128)(2,1)} %param.8) | copy-start | bytes 2654212
  7.2 158.1 %all-gather.2.cloned.1.call-start = ((), (), s32[]{:S(2)}) async-start(), calls=%async_computation | async-start | bytes 2433024 | tf_op jit(solution)/shard_map/all_gather | solution.py:59
  8.9 163.5 %collective-permute-start = (bf16[2,256,768]{2,1,0:T(8,128)(2,1)}, bf16[2,256,768]{2,1,0:T(8,128)(2,1)}, u32[]{:S(2)}, u32[]{:S(2)}) collective-permute-start(bf16[2,256,768]{2,1,0:T(8,128)(2,1)} %bitcast.53), channel_id=1, source_target_pairs={{1,0},{2,1},{3,2},{4,3},{5,4},{6,5},{7,6},{8,7},{9,8},{10,9},{11,1... | collective-permute-start | bytes 2359304 | tf_op jit(solution)/shard_map/ppermute | solution.py:11
  17.1 1.0 copy-start.2
  18.1 153.6 %copy-start.3 = (bf16[1,2,256,768]{3,2,1,0:T(8,128)(2,1)S(1)}, bf16[1,2,256,768]{3,2,1,0:T(8,128)(2,1)}, u32[]{:S(2)}) copy-start(bf16[1,2,256,768]{3,2,1,0:T(8,128)(2,1)} %param.11) | copy-start | bytes 2359300
  174.0 1.8 copy-start.4
  181.8 1.1 copy-start.1
  181.8 1.1 copy-start.5
  181.8 1.1 copy-start.6
  269.5 36.2 %collective-permute-start.1 = (bf16[16,1152]{1,0:T(8,128)(2,1)S(1)}, bf16[16,1152]{1,0:T(8,128)(2,1)S(1)}, u32[]{:S(2)}, u32[]{:S(2)}) collective-permute-start(bf16[16,1152]{1,0:T(8,128)(2,1)S(1)} %fusion), channel_id=1, source_target_pairs={{0,16},{16,32},{32,48},{48,64},{64,80},{80,96},{96,112},{112,128},... | collective-permute-start | bytes 110600
  271.4 37.6 %collective-permute-start.2 = (bf16[16,1152]{1,0:T(8,128)(2,1)S(1)}, bf16[16,1152]{1,0:T(8,128)(2,1)S(1)}, u32[]{:S(2)}, u32[]{:S(2)}) collective-permute-start(bf16[16,1152]{1,0:T(8,128)(2,1)S(1)} %fusion), channel_id=1, source_target_pairs={{0,32},{16,48},{32,64},{48,80},{64,96},{80,112},{96,128},{112,144}... | collective-permute-start | bytes 110600
  273.3 38.6 %collective-permute-start.3 = (bf16[16,1152]{1,0:T(8,128)(2,1)S(1)}, bf16[16,1152]{1,0:T(8,128)(2,1)S(1)}, u32[]{:S(2)}, u32[]{:S(2)}) collective-permute-start(bf16[16,1152]{1,0:T(8,128)(2,1)S(1)} %fusion), channel_id=1, source_target_pairs={{0,48},{16,64},{32,80},{48,96},{64,112},{80,128},{96,144},{112,160... | collective-permute-start | bytes 110600
  275.3 36.7 %collective-permute-start.4 = (bf16[16,1152]{1,0:T(8,128)(2,1)S(1)}, bf16[16,1152]{1,0:T(8,128)(2,1)S(1)}, u32[]{:S(2)}, u32[]{:S(2)}) collective-permute-start(bf16[16,1152]{1,0:T(8,128)(2,1)S(1)} %fusion), channel_id=1, source_target_pairs={{0,64},{16,80},{32,96},{48,112},{64,128},{80,144},{96,160},{112,17... | collective-permute-start | bytes 110600
  279.2 18.5 %collective-permute-start.8 = (bf16[12,1152]{1,0:T(8,128)(2,1)S(1)}, bf16[12,1152]{1,0:T(8,128)(2,1)S(1)}, u32[]{:S(2)}, u32[]{:S(2)}) collective-permute-start(bf16[12,1152]{1,0:T(8,128)(2,1)S(1)} %slice.34), channel_id=1, source_target_pairs={{0,128},{16,144},{32,160},{48,176},{64,192},{80,208},{96,224},{112... | collective-permute-start | bytes 82952
  297.7 14.3 %collective-permute-start.5 = (bf16[16,1152]{1,0:T(8,128)(2,1)S(1)}, bf16[16,1152]{1,0:T(8,128)(2,1)S(1)}, u32[]{:S(2)}, u32[]{:S(2)}) collective-permute-start(bf16[16,1152]{1,0:T(8,128)(2,1)S(1)} %fusion), channel_id=1, source_target_pairs={{0,80},{16,96},{32,112},{48,128},{64,144},{80,160},{96,176},{112,1... | collective-permute-start | bytes 110600
  305.7 15.7 %collective-permute-start.6 = (bf16[16,1152]{1,0:T(8,128)(2,1)S(1)}, bf16[16,1152]{1,0:T(8,128)(2,1)S(1)}, u32[]{:S(2)}, u32[]{:S(2)}) collective-permute-start(bf16[16,1152]{1,0:T(8,128)(2,1)S(1)} %fusion), channel_id=1, source_target_pairs={{0,96},{16,112},{32,128},{48,144},{64,160},{80,176},{96,192},{112,... | collective-permute-start | bytes 110600
  309.0 16.9 %collective-permute-start.7 = (bf16[16,1152]{1,0:T(8,128)(2,1)S(1)}, bf16[16,1152]{1,0:T(8,128)(2,1)S(1)}, u32[]{:S(2)}, u32[]{:S(2)}) collective-permute-start(bf16[16,1152]{1,0:T(8,128)(2,1)S(1)} %fusion), channel_id=1, source_target_pairs={{0,112},{16,128},{32,144},{48,160},{64,176},{80,192},{96,208},{112... | collective-permute-start | bytes 110600
Sparse Core Ops, SparseCore 0:
  11.7 153.5 all-gather.1
where the time goes:
time: 389 us; the launch traced here: 388 us
  waiting for transfers between devices  171 us (44%)
  blocking collectives  138 us (35%)
  starting transfers between devices  31.1 us (8%)
  matrix products  17.3 us (4%)
  between operations  15.6 us (4%)
  local copies, waits for them, and re-layouts  12.4 us (3%)
    all_gather x1, waiting for transfers between devices, on_device(): piece = lax.all_gather(time_weight, 'dp', axis=1, tiled=True)  147 us
    unnamed x2, blocking collectives  138 us
    unnamed x8, starting transfers between devices  29.8 us
    unnamed x9, waiting for transfers between devices  23.5 us
  transfers between devices with their start and end apart: 10, of which 4 were waited for; matrix products, arithmetic and copies ran while one was open for 4% of the time, Pallas kernels for 0%

commit v1 on v0

--- a/solution.py
+++ b/solution.py
@@ -56,7 +56,9 @@
     width = rows.shape[-1]
     incoming = passed_along(cotangent, "tm", -1)
     padded = jnp.concatenate([cotangent, incoming], 0)
-    piece = lax.all_gather(time_weight, "dp", axis=1, tiled=True)
+    piece = jnp.concatenate(
+        lax.all_to_all(jnp.stack([time_weight] * lax.axis_size("dp")), "dp", 0, 0), axis=1
+    )
     result = jnp.einsum(
         "fhd,cd->fhc", padded[2 : 2 + frames], piece[0], preferred_element_type=jnp.float32
     )

time: 389 us -> 345 us (0.89)
  waiting for transfers between devices: 171 us -> 116 us
  starting transfers between devices: 31.1 us -> 54.6 us
  between operations: 15.6 us -> 2.3 us
    all_gather x1 -> x0, waiting for transfers between devices: 147 us -> none  [on_device(): piece = lax.all_gather(time_weight, 'dp', axis=1, tiled=True)]
    all_to_all x0 -> x1, waiting for transfers between devices: none -> 95.4 us  [on_device(): lax.all_to_all(jnp.stack([time_weight] * lax.axis_size('dp')), 'dp', 0, 0)]
    all_to_all x0 -> x1, starting transfers between devices: none -> 18.4 us  [on_device(): lax.all_to_all(jnp.stack([time_weight] * lax.axis_size('dp')), 'dp', 0, 0)]
    unnamed x8, starting transfers between devices: 29.8 us -> 35 us
    slice x1, local copies, waits for them, and re-layouts: 6.43 us -> 1.47 us  [on_device(): piece[0]]
    unnamed x9 -> x8, waiting for transfers between devices: 23.5 us -> 20.1 us
  transfers between devices with their start and end apart: 10 -> 10, of which waited for: 4 -> 4; matrix products, arithmetic and copies ran while one was open for 4% -> 5% of each run, Pallas kernels for 0% -> 0%
where the time goes in v1:
time: 345 us; the launch traced here: 344 us
  blocking collectives  138 us (40%)
  waiting for transfers between devices  116 us (34%)
  starting transfers between devices  54.6 us (16%)
  matrix products  19.2 us (6%)
  local copies, waits for them, and re-layouts  11.1 us (3%)
  other arithmetic  3.94 us (1%)
    unnamed x2, blocking collectives  138 us
    all_to_all x1, waiting for transfers between devices, on_device(): lax.all_to_all(jnp.stack([time_weight] * lax.axis_size('dp')), 'dp', 0, 0)  95.4 us
    unnamed x8, starting transfers between devices  35 us
    unnamed x8, waiting for transfers between devices  20.1 us
    all_to_all x1, starting transfers between devices, on_device(): lax.all_to_all(jnp.stack([time_weight] * lax.axis_size('dp')), 'dp', 0, 0)  18.4 us
  transfers between devices with their start and end apart: 10, of which 4 were waited for; matrix products, arithmetic and copies ran while one was open for 5% of the time, Pallas kernels for 0%

profile of v1, /device:TPU:4, one launch (start us, length us, event | category | flops | bytes accessed | tf_op | source)
XLA Modules:
  0.0 344.5 jit_solution(7390792135793071628)
XLA Ops:
  0.6 0.0 copy-start
  0.6 2.5 stack.2
  3.2 18.4 %all-to-all-start = ((bf16[32,3,12,768]{3,2,1,0:T(8,128)(2,1)}), bf16[32,3,12,768]{3,2,1,0:T(8,128)(2,1)S(1)}, u32[]{:S(2)}, u32[]{:S(2)}) async-start(bf16[32,3,12,768]{3,2,1,0:T(8,128)(2,1)} %stack.2), calls=%async_computation | async-start | bytes 4718592 | tf_op jit(solution)/shard_map/all_to_all | solution.py:60
  21.5 1.3 collective-permute-start
  22.8 1.3 dynamic-slice.6
  24.8 1.3 dynamic-slice.2
  26.7 1.1 fusion.16
  27.8 0.0 copy-done
  27.9 0.0 copy-done.11
  27.9 1.9 convolution_convert_fusion
  29.8 0.0 copy-start.6
  29.8 0.3 convolution_multiply_fusion.1
  30.1 0.0 copy-start.4
  30.1 1.1 fusion.38
  31.2 0.0 copy-done.6
  31.2 0.0 copy-done.4
  31.2 95.4 %all-to-all-done = bf16[32,3,12,768]{3,2,1,0:T(8,128)(2,1)S(1)} async-done(((bf16[32,3,12,768]{3,2,1,0:T(8,128)(2,1)}), bf16[32,3,12,768]{3,2,1,0:T(8,128)(2,1)S(1)}, u32[]{:S(2)}, u32[]{:S(2)}) %all-to-all-start) | async-done | bytes 1769504 | tf_op jit(solution)/shard_map/all_to_all | solution.py:60
  126.6 1.5 fusion.37
  128.1 2.1 reshape.52
  130.2 0.0 copy-done.2
  130.2 0.1 reshape.53
  130.3 0.0 copy-done.1
  130.3 0.1 reshape.51
  130.5 0.0 copy-start.8
  130.5 0.0 copy-start.9
  130.5 1.8 fusion.33
  132.3 0.0 collective-permute-done
  132.3 0.0 copy-done.8
  132.3 0.0 copy-done.9
  132.4 1.6 fusion.3
  133.9 0.0 copy-start.10
  134.0 0.0 copy-start.7
  134.0 1.8 fusion.9
  135.8 0.0 copy-done.10
  135.8 0.0 copy-start.3
  135.8 0.4 convolution_convert_fusion.4
  136.2 0.6 copy-done.3
  136.9 0.3 multiply_reduce_fusion
  137.2 2.3 convolution_convert_fusion.2
  139.5 2.4 convolution_convert_fusion.1
  141.9 2.4 convolution_convert_fusion.3
  144.3 1.9 fusion.2
  146.2 84.8 %fusion = bf16[16,1152]{1,0:T(8,128)(2,1)S(1)} fusion(bf16[384,1152]{1,0:T(8,128)(2,1)S(1)} %fusion.2), kind=kCustom, calls=%all-reduce-scatter | all-reduce-scatter fusion | flops 589825 | bytes 923648
  231.1 3.5 %collective-permute-start.1 = (bf16[16,1152]{1,0:T(8,128)(2,1)S(1)}, bf16[16,1152]{1,0:T(8,128)(2,1)S(1)}, u32[]{:S(2)}, u32[]{:S(2)}) collective-permute-start(bf16[16,1152]{1,0:T(8,128)(2,1)S(1)} %fusion), channel_id=1, source_target_pairs={{0,16},{16,32},{32,48},{48,64},{64,80},{80,96},{96,112},{112,128},... | collective-permute-start | bytes 110600
  234.5 1.9 collective-permute-start.2
  236.5 1.9 collective-permute-start.3
  238.4 1.9 collective-permute-start.4
  240.3 2.0 fusion.19
  242.4 10.7 %collective-permute-start.8 = (bf16[12,1152]{1,0:T(8,128)(2,1)S(1)}, bf16[12,1152]{1,0:T(8,128)(2,1)S(1)}, u32[]{:S(2)}, u32[]{:S(2)}) collective-permute-start(bf16[12,1152]{1,0:T(8,128)(2,1)S(1)} %slice.37), channel_id=1, source_target_pairs={{0,128},{16,144},{32,160},{48,176},{64,192},{80,208},{96,224},{112... | collective-permute-start | bytes 82952
  253.1 7.0 %collective-permute-done.8 = bf16[12,1152]{1,0:T(8,128)(2,1)S(1)} collective-permute-done((bf16[12,1152]{1,0:T(8,128)(2,1)S(1)}, bf16[12,1152]{1,0:T(8,128)(2,1)S(1)}, u32[]{:S(2)}, u32[]{:S(2)}) %collective-permute-start.8) | collective-permute-done | bytes 27680
  260.1 10.7 %collective-permute-start.5 = (bf16[16,1152]{1,0:T(8,128)(2,1)S(1)}, bf16[16,1152]{1,0:T(8,128)(2,1)S(1)}, u32[]{:S(2)}, u32[]{:S(2)}) collective-permute-start(bf16[16,1152]{1,0:T(8,128)(2,1)S(1)} %fusion), channel_id=1, source_target_pairs={{0,80},{16,96},{32,112},{48,128},{64,144},{80,160},{96,176},{112,1... | collective-permute-start | bytes 110600
  270.8 0.0 collective-permute-done.1
  270.9 2.4 collective-permute-start.6
  273.2 0.0 collective-permute-done.2
  273.3 1.9 collective-permute-start.7
  275.2 1.0 fusion.20
  276.2 0.0 collective-permute-done.3
  276.2 0.0 collective-permute-done.4
  276.2 0.0 collective-permute-done.5
  276.2 9.8 %collective-permute-done.6 = bf16[16,1152]{1,0:T(8,128)(2,1)S(1)} collective-permute-done((bf16[16,1152]{1,0:T(8,128)(2,1)S(1)}, bf16[16,1152]{1,0:T(8,128)(2,1)S(1)}, u32[]{:S(2)}, u32[]{:S(2)}) %collective-permute-start.6) | collective-permute-done | bytes 36896
  286.0 3.3 collective-permute-done.7
  289.3 1.5 concatenate.4
  290.8 53.0 %all-reduce.4 = bf16[12,1152]{1,0:T(8,128)(2,1)S(1)} all-reduce(bf16[12,1152]{1,0:T(8,128)(2,1)S(1)} %constant_dynamic-slice_fusion), channel_id=3, replica_groups=mesh['dp'=32,'tm'=16] {'tm'}, use_global_device_ids=true, to_apply=%region_6.0.clone | all-reduce | flops 13824 | bytes 55296
  343.8 0.7 dynamic-slice_convert_fusion
  (14 shorter events, 0.1 us)
Async XLA Ops:
  0.6 27.2 %copy-start = (bf16[384,1152]{1,0:T(8,128)(2,1)S(1)}, bf16[384,1152]{1,0:T(8,128)(2,1)}, u32[]{:S(2)}) copy-start(bf16[384,1152]{1,0:T(8,128)(2,1)} %param.8) | copy-start | bytes 2654212
  3.2 24.7 %copy-start.11 = (f32[384]{0:T(512)S(1)}, f32[384]{0:T(512)}, u32[]{:S(2)}) copy-start(f32[384]{0:T(512)} %param.7) | copy-start | bytes 4612
  3.2 123.4 %all-to-all-start = ((bf16[32,3,12,768]{3,2,1,0:T(8,128)(2,1)}), bf16[32,3,12,768]{3,2,1,0:T(8,128)(2,1)S(1)}, u32[]{:S(2)}, u32[]{:S(2)}) async-start(bf16[32,3,12,768]{3,2,1,0:T(8,128)(2,1)} %stack.2), calls=%async_computation | async-start | bytes 4718592 | tf_op jit(solution)/shard_map/all_to_all | solution.py:60
  21.5 110.8 %collective-permute-start = (bf16[2,256,768]{2,1,0:T(8,128)(2,1)}, bf16[2,256,768]{2,1,0:T(8,128)(2,1)}, u32[]{:S(2)}, u32[]{:S(2)}) collective-permute-start(bf16[2,256,768]{2,1,0:T(8,128)(2,1)} %bitcast.52), channel_id=1, source_target_pairs={{1,0},{2,1},{3,2},{4,3},{5,4},{6,5},{7,6},{8,7},{9,8},{10,9},{11,1... | collective-permute-start | bytes 2359304 | tf_op jit(solution)/shard_map/ppermute | solution.py:11
  29.8 1.4 copy-start.6
  30.1 1.1 copy-start.4
  128.0 2.1 copy-start.2
  128.1 2.3 copy-start.1
  130.5 1.9 copy-start.8
  130.5 1.9 copy-start.9
  133.9 1.9 copy-start.10
  134.0 2.3 copy-start.7
  135.8 1.0 copy-start.3
  141.9 2.4 copy-start.5
  141.9 2.4 copy-start.12
  231.1 39.8 %collective-permute-start.1 = (bf16[16,1152]{1,0:T(8,128)(2,1)S(1)}, bf16[16,1152]{1,0:T(8,128)(2,1)S(1)}, u32[]{:S(2)}, u32[]{:S(2)}) collective-permute-start(bf16[16,1152]{1,0:T(8,128)(2,1)S(1)} %fusion), channel_id=1, source_target_pairs={{0,16},{16,32},{32,48},{48,64},{64,80},{80,96},{96,112},{112,128},... | collective-permute-start | bytes 110600
  234.5 38.7 %collective-permute-start.2 = (bf16[16,1152]{1,0:T(8,128)(2,1)S(1)}, bf16[16,1152]{1,0:T(8,128)(2,1)S(1)}, u32[]{:S(2)}, u32[]{:S(2)}) collective-permute-start(bf16[16,1152]{1,0:T(8,128)(2,1)S(1)} %fusion), channel_id=1, source_target_pairs={{0,32},{16,48},{32,64},{48,80},{64,96},{80,112},{96,128},{112,144}... | collective-permute-start | bytes 110600
  236.5 39.7 %collective-permute-start.3 = (bf16[16,1152]{1,0:T(8,128)(2,1)S(1)}, bf16[16,1152]{1,0:T(8,128)(2,1)S(1)}, u32[]{:S(2)}, u32[]{:S(2)}) collective-permute-start(bf16[16,1152]{1,0:T(8,128)(2,1)S(1)} %fusion), channel_id=1, source_target_pairs={{0,48},{16,64},{32,80},{48,96},{64,112},{80,128},{96,144},{112,160... | collective-permute-start | bytes 110600
  238.4 37.8 %collective-permute-start.4 = (bf16[16,1152]{1,0:T(8,128)(2,1)S(1)}, bf16[16,1152]{1,0:T(8,128)(2,1)S(1)}, u32[]{:S(2)}, u32[]{:S(2)}) collective-permute-start(bf16[16,1152]{1,0:T(8,128)(2,1)S(1)} %fusion), channel_id=1, source_target_pairs={{0,64},{16,80},{32,96},{48,112},{64,128},{80,144},{96,160},{112,17... | collective-permute-start | bytes 110600
  242.4 17.7 %collective-permute-start.8 = (bf16[12,1152]{1,0:T(8,128)(2,1)S(1)}, bf16[12,1152]{1,0:T(8,128)(2,1)S(1)}, u32[]{:S(2)}, u32[]{:S(2)}) collective-permute-start(bf16[12,1152]{1,0:T(8,128)(2,1)S(1)} %slice.37), channel_id=1, source_target_pairs={{0,128},{16,144},{32,160},{48,176},{64,192},{80,208},{96,224},{112... | collective-permute-start | bytes 82952
  260.1 16.1 %collective-permute-start.5 = (bf16[16,1152]{1,0:T(8,128)(2,1)S(1)}, bf16[16,1152]{1,0:T(8,128)(2,1)S(1)}, u32[]{:S(2)}, u32[]{:S(2)}) collective-permute-start(bf16[16,1152]{1,0:T(8,128)(2,1)S(1)} %fusion), channel_id=1, source_target_pairs={{0,80},{16,96},{32,112},{48,128},{64,144},{80,160},{96,176},{112,1... | collective-permute-start | bytes 110600
  270.9 15.2 %collective-permute-start.6 = (bf16[16,1152]{1,0:T(8,128)(2,1)S(1)}, bf16[16,1152]{1,0:T(8,128)(2,1)S(1)}, u32[]{:S(2)}, u32[]{:S(2)}) collective-permute-start(bf16[16,1152]{1,0:T(8,128)(2,1)S(1)} %fusion), channel_id=1, source_target_pairs={{0,96},{16,112},{32,128},{48,144},{64,160},{80,176},{96,192},{112,... | collective-permute-start | bytes 110600
  273.3 16.1 %collective-permute-start.7 = (bf16[16,1152]{1,0:T(8,128)(2,1)S(1)}, bf16[16,1152]{1,0:T(8,128)(2,1)S(1)}, u32[]{:S(2)}, u32[]{:S(2)}) collective-permute-start(bf16[16,1152]{1,0:T(8,128)(2,1)S(1)} %fusion), channel_id=1, source_target_pairs={{0,112},{16,128},{32,144},{48,160},{64,176},{80,192},{96,208},{112... | collective-permute-start | bytes 110600
